TPU v7x, 256 devices: a whole 4x4x8 slice. The times are simulated.
256 devices in a mesh: frame: 64 (over y, z, core), text: 4 (over x).
Axes of the slice: x: 4, y: 4, z: 8, core: 2. Of those that a mesh axis runs over, the one named last changes fastest.
Arguments:
- frame_keys: bfloat16 [32768, 4096], P('frame', 'text'), may hold values from -6 to 6
- frame_values: bfloat16 [32768, 4096], P('frame', 'text'), may hold values from -6 to 6
- frame_grads: bfloat16 [32768, 4096], P('frame', 'text'), may hold values from -6 to 6
- text_keys: bfloat16 [8192, 4096], P(('frame', 'text')), may hold values from -6 to 6
- text_values: bfloat16 [8192, 4096], P(('frame', 'text')), may hold values from -6 to 6
- text_grads: bfloat16 [8192, 4096], P(('frame', 'text')), may hold values from -6 to 6
- band_first: int32 [256], P('frame'), may hold values from 0 to 63, as said below
- band_count: int32 [256], P('frame'), may hold values from 1 to 3
Outputs:
- frame_out: bfloat16 [32768, 4096], P('frame', 'text')
- text_out: bfloat16 [8192, 4096], P('frame', 'text')
- frame_key_grad: bfloat16 [32768, 4096], P('frame', 'text')
- frame_value_grad: bfloat16 [32768, 4096], P('frame', 'text')
- text_key_grad: bfloat16 [8192, 4096], P('frame', 'text')
- text_value_grad: bfloat16 [8192, 4096], P('frame', 'text')
Inputs may be any that keep to these rules, and one draw needn't show every extreme that they name: For frame block b, band_first[b] is b // 4 - 1 or b // 4, and band_first[b] + band_count[b] - 1 is b // 4 or b // 4 + 1, so every text block lies in some band.
All inputs are finite; a program needn't handle non-finite values.
Results may differ from a plain program's by a relative error of at most 0.023.
Values may be sent and summed in bfloat16 or wider, within the bound.
A program may use at most 128 MiB of HBM per device.

v0:
```python
import functools
import math
import jax
import jax.numpy as jnp
from jax import lax
from jax.sharding import PartitionSpec as P

HEAD_DIM = 128
BLOCK = 128
NEGATIVE = -1e30


def extended(array, sides, width):
    for axis, dim in sides:
        size, length = (lax.axis_size(axis), array.shape[dim])
        up = [(i, (i + 1) % size) for i in range(size - 1)]
        down = [(j, i) for i, j in up]
        last = lax.slice_in_dim(array, length - width, length, axis=dim)
        initial = lax.slice_in_dim(array, 0, width, axis=dim)
        before = lax.ppermute(last, axis, up)
        after = lax.ppermute(initial, axis, down)
        array = jnp.concatenate([before, array, after], axis=dim)
    return array


def from_behind(block, axis, distance):
    devices = range(lax.axis_size(axis))
    route = [(i - distance, i) for i in devices if i - distance in devices]
    return lax.ppermute(block, axis, route)


def block_mask(first_ids, count_ids, text_ids):
    lower = first_ids[:, None]
    upper = lower + count_ids[:, None]
    inside = (text_ids[None, :] >= lower) & (text_ids[None, :] < upper)
    row_blocks, col_blocks = inside.shape
    grown = jnp.broadcast_to(inside[:, None, :, None], (row_blocks, BLOCK, col_blocks, BLOCK))
    return grown.reshape(row_blocks * BLOCK, col_blocks * BLOCK)


def on_device(
    frame_keys,
    frame_values,
    frame_grads,
    text_keys,
    text_values,
    text_grads,
    band_first,
    band_count,
):
    score_scale = 1.0 / math.sqrt(HEAD_DIM)
    stacked = jnp.stack([text_keys, text_values, text_grads])
    group_count = lax.axis_size("text")
    rows_sub = stacked.shape[1]
    window = extended(stacked, (("frame", 1),), rows_sub)
    arrived = lax.all_to_all(window, "text", split_axis=2, concat_axis=1, tiled=True)
    head_width = arrived.shape[2]
    arrived = arrived.reshape(3, group_count, 3, rows_sub, head_width).transpose(0, 2, 1, 3, 4)
    own_rows = group_count * rows_sub
    arrived = arrived.reshape(3, 3 * own_rows, head_width)
    own_text = arrived[:, own_rows : 2 * own_rows]
    head_count = frame_keys.shape[1] // HEAD_DIM
    frame_rows = frame_keys.shape[0]
    win_rows = 3 * own_rows
    keys_win = arrived[0].reshape(win_rows, head_count, HEAD_DIM)
    values_win = arrived[1].reshape(win_rows, head_count, HEAD_DIM)
    grads_win = arrived[2].reshape(win_rows, head_count, HEAD_DIM)
    own_grads_text = own_text[2].reshape(own_rows, head_count, HEAD_DIM)
    frame_k = frame_keys.reshape(frame_rows, head_count, HEAD_DIM)
    frame_v = frame_values.reshape(frame_rows, head_count, HEAD_DIM)
    frame_g = frame_grads.reshape(frame_rows, head_count, HEAD_DIM)
    frame_index = lax.axis_index("frame")
    text_per_dev = own_rows // BLOCK
    text_ids = (frame_index - 1) * text_per_dev + jnp.arange(3 * text_per_dev, dtype=jnp.int32)
    live_pairs = block_mask(band_first, band_count, text_ids)[None]
    scores = score_scale * jnp.einsum(
        "fhd,thd->hft", frame_k, keys_win, preferred_element_type=jnp.float32
    )
    row_max = jnp.max(jnp.where(live_pairs, scores, NEGATIVE), axis=2)
    row_exp = jnp.exp(jnp.where(live_pairs, scores - row_max[:, :, None], NEGATIVE))
    row_total = jnp.sum(row_exp, axis=2)
    row_probs = row_exp / row_total[:, :, None]
    row_low = row_probs.astype(jnp.bfloat16)
    frame_out = jnp.einsum(
        "hft,thd->fhd", row_low, values_win, preferred_element_type=jnp.float32
    ).astype(jnp.bfloat16)
    frame_dot = jnp.sum(frame_g.astype(jnp.float32) * frame_out.astype(jnp.float32), axis=2).T
    col_max = jnp.max(jnp.where(live_pairs, scores, NEGATIVE), axis=1)
    col_exp = jnp.exp(jnp.where(live_pairs, scores - col_max[:, None, :], NEGATIVE))
    col_total = jnp.sum(col_exp, axis=1)
    col_weights = col_exp.astype(jnp.bfloat16)
    col_sum = jnp.einsum("hft,fhd->thd", col_weights, frame_v, preferred_element_type=jnp.float32)
    own_slice = slice(own_rows, 2 * own_rows)
    members = [(col_max[:, own_slice], col_total[:, own_slice], col_sum[own_slice])]
    for offset, segment in ((-1, 0), (1, 2)):
        window_slice = slice(segment * own_rows, (segment + 1) * own_rows)
        members.append(
            from_behind(
                (col_max[:, window_slice], col_total[:, window_slice], col_sum[window_slice]),
                "frame",
                offset,
            )
        )
    safe_max = [jnp.where(member[1] > 0, member[0], NEGATIVE) for member in members]
    column_peak = functools.reduce(jnp.maximum, safe_max)
    factors = [jnp.exp(partial_max - column_peak) for partial_max in safe_max]
    column_total = functools.reduce(
        jnp.add, [member[1] * factor for member, factor in zip(members, factors)]
    )
    column_sum = functools.reduce(
        jnp.add, [member[2] * factor.T[:, :, None] for member, factor in zip(members, factors)]
    )
    text_out = (column_sum / column_total.T[:, :, None]).astype(jnp.bfloat16)
    text_dot = jnp.sum(own_grads_text.astype(jnp.float32) * text_out.astype(jnp.float32), axis=2).T
    stats_win = (
        extended(column_peak, (("frame", 1),), own_rows),
        extended(column_total, (("frame", 1),), own_rows),
        extended(text_dot, (("frame", 1),), own_rows),
    )
    win_max, win_total, win_dot = stats_win
    win_total = jnp.where(win_total > 0, win_total, 1.0)
    col_probs = (
        jnp.exp(jnp.where(live_pairs, scores - win_max[:, None, :], NEGATIVE))
        / win_total[:, None, :]
    )
    grad_rows = jnp.einsum("fhd,thd->hft", frame_g, values_win, preferred_element_type=jnp.float32)
    grad_cols = jnp.einsum("fhd,thd->hft", frame_v, grads_win, preferred_element_type=jnp.float32)
    grad_score = (
        row_probs * (grad_rows - frame_dot[:, :, None])
        + col_probs * (grad_cols - win_dot[:, None, :])
    ).astype(jnp.bfloat16)
    frame_key_grad = (
        score_scale
        * jnp.einsum("hft,thd->fhd", grad_score, keys_win, preferred_element_type=jnp.float32)
    ).astype(jnp.bfloat16)
    frame_value_grad = jnp.einsum(
        "hft,thd->fhd",
        col_probs.astype(jnp.bfloat16),
        grads_win,
        preferred_element_type=jnp.float32,
    ).astype(jnp.bfloat16)
    key_terms = score_scale * jnp.einsum(
        "hft,fhd->thd", grad_score, frame_k, preferred_element_type=jnp.float32
    )
    value_terms = jnp.einsum("hft,fhd->thd", row_low, frame_g, preferred_element_type=jnp.float32)
    key_total = key_terms[own_slice]
    value_total = value_terms[own_slice]
    for offset, segment in ((-1, 0), (1, 2)):
        window_slice = slice(segment * own_rows, (segment + 1) * own_rows)
        returned = (
            from_behind(key_terms[window_slice].astype(jnp.bfloat16), "frame", offset).astype(
                jnp.float32
            ),
            from_behind(value_terms[window_slice].astype(jnp.bfloat16), "frame", offset).astype(
                jnp.float32
            ),
        )
        key_total = key_total + returned[0]
        value_total = value_total + returned[1]
    out_width = head_count * HEAD_DIM
    return (
        frame_out.reshape(frame_rows, out_width),
        text_out.reshape(own_rows, out_width),
        frame_key_grad.reshape(frame_rows, out_width),
        frame_value_grad.reshape(frame_rows, out_width),
        key_total.astype(jnp.bfloat16).reshape(own_rows, out_width),
        value_total.astype(jnp.bfloat16).reshape(own_rows, out_width),
    )


def solution(mesh):
    in_specs = (
        P("frame", "text"),
        P("frame", "text"),
        P("frame", "text"),
        P(("frame", "text"), None),
        P(("frame", "text"), None),
        P(("frame", "text"), None),
        P("frame"),
        P("frame"),
    )
    out_specs = (
        P("frame", "text"),
        P("frame", "text"),
        P("frame", "text"),
        P("frame", "text"),
        P("frame", "text"),
        P("frame", "text"),
    )
    return jax.shard_map(
        on_device, mesh=mesh, in_specs=in_specs, out_specs=out_specs, check_vma=False
    )
```

profile of v0, /device:TPU:24, one launch (start us, length us, event | category | flops | bytes accessed | tf_op | source)
XLA Modules:
  0.0 224.5 jit_solution(12583766159716517799)
XLA Ops:
  1.9 7.4 %collective-permute-start.1 = (bf16[3,32,4096]{2,1,0:T(8,128)(2,1)S(1)}, bf16[3,32,4096]{2,1,0:T(8,128)(2,1)S(1)}, u32[]{:S(2)}, u32[]{:S(2)}) collective-permute-start(bf16[3,32,4096]{2,1,0:T(8,128)(2,1)S(1)} %pad_maximum_fusion.1), channel_id=1, source_target_pairs={{4,0},{8,4},{12,8},{16,12},{20,16},{24,20},{28,24},{32,28},{36,32}... | collective-permute-start | bytes 2359304 | tf_op jit(solution)/shard_map/ppermute | solution.py:21
  11.3 7.6 %collective-permute-done.1 = bf16[3,32,4096]{2,1,0:T(8,128)(2,1)S(1)} collective-permute-done((bf16[3,32,4096]{2,1,0:T(8,128)(2,1)S(1)}, bf16[3,32,4096]{2,1,0:T(8,128)(2,1)S(1)}, u32[]{:S(2)}, u32[]{:S(2)}) %collective-permute-start.1) | collective-permute-done | bytes 786464 | tf_op jit(solution)/shard_map/ppermute | solution.py:21
  18.8 5.9 %collective-permute-done = bf16[3,32,4096]{2,1,0:T(8,128)(2,1)S(1)} collective-permute-done((bf16[3,32,4096]{2,1,0:T(8,128)(2,1)S(1)}, bf16[3,32,4096]{2,1,0:T(8,128)(2,1)S(1)}, u32[]{:S(2)}, u32[]{:S(2)}) %collective-permute-start) | collective-permute-done | bytes 786464 | tf_op jit(solution)/shard_map/ppermute | solution.py:20
  26.1 4.8 %copy.128 = bf16[3,96,4096]{1,0,2:T(4,128)(2,1)} copy(bf16[3,96,4096]{2,1,0:T(8,128)(2,1)S(1)} %pad_maximum_fusion) | data formatting | bytes 4718592 | tf_op jit(solution)/shard_map/concatenate | solution.py:22
  30.9 5.0 %all-to-all-start = ((bf16[3,96,4096]{1,0,2:T(4,128)(2,1)}), bf16[3,96,4096]{1,0,2:T(4,128)(2,1)}, u32[]{:S(2)}, u32[]{:S(2)}) async-start(bf16[3,96,4096]{1,0,2:T(4,128)(2,1)} %copy.128), calls=%async_computation | async-start | bytes 8388608 | tf_op jit(solution)/shard_map/all_to_all | solution.py:56
  39.6 37.6 %all-to-all-done = bf16[3,96,4096]{1,0,2:T(4,128)(2,1)} async-done(((bf16[3,96,4096]{1,0,2:T(4,128)(2,1)}), bf16[3,96,4096]{1,0,2:T(4,128)(2,1)}, u32[]{:S(2)}, u32[]{:S(2)}) %all-to-all-start) | async-done | bytes 2359328 | tf_op jit(solution)/shard_map/all_to_all | solution.py:56
  77.2 5.5 %copy.130 = bf16[3,4,96,1024]{3,2,1,0:T(8,128)(2,1)S(1)} copy(bf16[3,4,96,1024]{2,0,3,1:T(4,128)(2,1)} %bitcast.5) | data formatting | bytes 4718592 | tf_op jit(solution)/shard_map/all_to_all | solution.py:56
  88.5 5.5 %fusion.10 = (f32[8,384]{1,0:T(8,128)S(1)}, f32[8,384,512]{2,1,0:T(8,128)}) fusion(pred[512,384]{0,1:T(8,128)(4,1)} %bitcast.162, bf16[384,8,128]{0,2,1:T(8,128)(2,1)S(1)} %copy.147, bf16[512,8,128]{0,2,1:T(8,128)(2,1)} %bitcast.144), kind=kOutput, calls=%fused_computation.16 | convolution fusion | flops 407368704 | bytes 8335360 | tf_op jit(solution)/shard_map/fhd,thd->hft/dot_general | solution.py:76
  94.0 5.8 %fusion.67 = (f32[8,512]{1,0:T(8,128)S(1)}, f32[8,512,384]{1,2,0:T(8,128)}) fusion(pred[512,384]{0,1:T(8,128)(4,1)S(1)} %bitcast.164, bf16[384,8,128]{0,2,1:T(8,128)(2,1)S(1)} %copy.147, bf16[512,8,128]{0,2,1:T(8,128)(2,1)S(1)} %bitcast.145), kind=kOutput, calls=%fused_computation.92 | convolution fusion | flops 814743936 | bytes 8339456 | tf_op jit(solution)/shard_map/sub | solution.py:80
  102.2 2.4 %copy.149 = bf16[384,8,128]{0,2,1:T(8,128)(2,1)} copy(bf16[384,8,128]{2,1,0:T(8,128)(2,1)} %bitcast.156) | data formatting | bytes 1572864 | tf_op jit(solution)/shard_map/reshape;squeeze | solution.py:67
  106.0 4.3 %fusion.12 = f32[8,384]{1,0:T(8,128)S(1)} fusion(f32[8,384,512]{2,1,0:T(8,128)} %get-tuple-element.59, f32[8,384]{1,0:T(8,128)S(1)} %get-tuple-element.58, pred[512,384]{0,1:T(8,128)(4,1)S(1)} %bitcast.165), kind=kLoop, calls=%fused_computation.18 | loop fusion | flops 6288384 | bytes 6512640 | tf_op jit(solution)/shard_map/reduce_sum | solution.py:90
  112.4 3.6 %fusion.34 = f32[8,384,512]{2,1,0:T(8,128)} fusion(bf16[384,8,128]{0,2,1:T(8,128)(2,1)S(1)} %copy-done.9, bf16[512,1024]{1,0:T(8,128)(2,1)S(1)} %copy-done), kind=kOutput, calls=%fused_computation.42 | convolution fusion | flops 402653184 | bytes 8126464 | tf_op jit(solution)/shard_map/fhd,thd->hft/dot_general | solution.py:127
  116.0 9.2 %collective-permute-start.2 = (f32[8,128]{1,0:T(8,128)S(1)}, f32[8,128]{1,0:T(8,128)S(1)}, u32[]{:S(2)}, u32[]{:S(2)}) collective-permute-start(f32[8,128]{1,0:T(8,128)S(1)} %get-tuple-element.54), channel_id=1, source_target_pairs={{4,0},{8,4},{12,8},{16,12},{20,16},{24,20},{28,24},{32,28},{36,32}... | collective-permute-start | bytes 12296 | tf_op jit(solution)/shard_map/ppermute | solution.py:29
  127.2 5.8 %collective-permute-start.3 = (f32[8,128]{1,0:T(8,128)S(1)}, f32[8,128]{1,0:T(8,128)S(1)}, u32[]{:S(2)}, u32[]{:S(2)}) collective-permute-start(f32[8,128]{1,0:T(8,128)S(1)} %get-tuple-element.52), channel_id=1, source_target_pairs={{4,0},{8,4},{12,8},{16,12},{20,16},{24,20},{28,24},{32,28},{36,32}... | collective-permute-start | bytes 12296 | tf_op jit(solution)/shard_map/ppermute | solution.py:29
  135.9 5.9 %collective-permute-start.6 = (f32[128,8,128]{0,2,1:T(8,128)}, f32[128,8,128]{0,2,1:T(8,128)}, u32[]{:S(2)}, u32[]{:S(2)}) collective-permute-start(f32[128,8,128]{0,2,1:T(8,128)} %get-tuple-element.43), channel_id=1, source_target_pairs={{4,0},{8,4},{12,8},{16,12},{20,16},{24,20},{28,24},{32,28},{36,32}... | collective-permute-start | bytes 1572872 | tf_op jit(solution)/shard_map/ppermute | solution.py:29
  148.9 5.8 %collective-permute-start.11 = (f32[8,128]{1,0:T(8,128)S(1)}, f32[8,128]{1,0:T(8,128)S(1)}, u32[]{:S(2)}, u32[]{:S(2)}) collective-permute-start(f32[8,128]{1,0:T(8,128)S(1)} %get-tuple-element.50), channel_id=1, source_target_pairs={{4,0},{8,4},{12,8},{16,12},{20,16},{24,20},{28,24},{32,28},{36,32}... | collective-permute-start | bytes 12296 | tf_op jit(solution)/shard_map/ppermute | solution.py:21
  159.9 5.7 %collective-permute-start.16 = (bf16[128,8,128]{0,2,1:T(8,128)(2,1)}, bf16[128,8,128]{0,2,1:T(8,128)(2,1)}, u32[]{:S(2)}, u32[]{:S(2)}) collective-permute-start(bf16[128,8,128]{0,2,1:T(8,128)(2,1)} %get-tuple-element.45), channel_id=1, source_target_pairs={{4,0},{8,4},{12,8},{16,12},{20,16},{24,20},{28,24},{32,28},{36,32}... | collective-permute-start | bytes 786440 | tf_op jit(solution)/shard_map/ppermute | solution.py:29
  167.6 5.8 %collective-permute-start.9 = (f32[8,128]{1,0:T(8,128)S(1)}, f32[8,128]{1,0:T(8,128)S(1)}, u32[]{:S(2)}, u32[]{:S(2)}) collective-permute-start(f32[8,128]{1,0:T(8,128)S(1)} %get-tuple-element.39), channel_id=1, source_target_pairs={{4,0},{8,4},{12,8},{16,12},{20,16},{24,20},{28,24},{32,28},{36,32}... | collective-permute-start | bytes 12296 | tf_op jit(solution)/shard_map/ppermute | solution.py:21
  175.3 6.3 %fusion.27 = bf16[8,128,512]{2,1,0:T(8,128)(2,1)} fusion(bf16[384,8,128]{0,2,1:T(8,128)(2,1)S(1)} %copy-done.10, f32[8,384,512]{2,1,0:T(8,128)} %get-tuple-element.59, f32[8,384]{1,0:T(8,128)S(1)} %compare_select_fusion, f32[8,384]{1,0:T(8,128)S(1)} %pad_maximum_fusion.2, pred[512,384]{0,1:T(8,128)(4,1)} %bitcast.163), kind=kOutput, calls=%fused_computation.37 | convolution fusion | flops 411041792 | bytes 8347648 | tf_op jit(solution)/shard_map/hft,thd->fhd/dot_general | solution.py:136
  181.6 2.3 %copy.157 = bf16[512,1024]{1,0:T(8,128)(2,1)} copy(bf16[512,1024]{0,1:T(8,128)(2,1)} %bitcast.171) | data formatting | bytes 2097152
  185.6 5.8 %collective-permute-start.13 = (f32[8,128]{1,0:T(8,128)S(1)}, f32[8,128]{1,0:T(8,128)S(1)}, u32[]{:S(2)}, u32[]{:S(2)}) collective-permute-start(f32[8,128]{1,0:T(8,128)S(1)} %bitcast.181), channel_id=1, source_target_pairs={{4,0},{8,4},{12,8},{16,12},{20,16},{24,20},{28,24},{32,28},{36,32}... | collective-permute-start | bytes 12296 | tf_op jit(solution)/shard_map/ppermute | solution.py:21
  198.4 8.2 %fusion.2 = bf16[8,512,384]{1,2,0:T(8,128)(2,1)S(1)} fusion(f32[8,384,512]{2,1,0:T(8,128)} %fusion.34, f32[8,384]{1,0:T(8,128)S(1)} %pad_maximum_fusion.3, f32[8,512]{1,0:T(8,128)S(1)} %bitcast.180, bf16[512,8,128]{0,2,1:T(8,128)(2,1)S(1)} %bitcast.148, f32[8,512,384]{1,2,0:T(8,128)} %get-tuple-element.57, f32[8,512]{1,0:T(8,128)S(1)} %get-tuple-element.56, ...), kind=kOutput, calls=%fused_computation.3 | convolution fusion | flops 419954688 | bytes 24121344 | tf_op jit(solution)/shard_map/fhd,thd->hft/dot_general | solution.py:126
  209.0 3.7 %collective-permute-start.14 = (bf16[128,8,128]{0,2,1:T(8,128)(2,1)S(1)}, bf16[128,8,128]{0,2,1:T(8,128)(2,1)S(1)}, u32[]{:S(2)}, u32[]{:S(2)}) collective-permute-start(bf16[128,8,128]{0,2,1:T(8,128)(2,1)S(1)} %get-tuple-element.47), channel_id=1, source_target_pairs={{4,0},{8,4},{12,8},{16,12},{20,16},{24,20},{28,24},{32,28},{36,32}... | collective-permute-start | bytes 786440 | tf_op jit(solution)/shard_map/ppermute | solution.py:29
  216.7 5.8 %collective-permute-done.15 = bf16[128,8,128]{0,2,1:T(8,128)(2,1)S(1)} collective-permute-done((bf16[128,8,128]{0,2,1:T(8,128)(2,1)S(1)}, bf16[128,8,128]{0,2,1:T(8,128)(2,1)S(1)}, u32[]{:S(2)}, u32[]{:S(2)}) %collective-permute-start.15) | collective-permute-done | bytes 262176 | tf_op jit(solution)/shard_map/ppermute | solution.py:29
  (116 shorter events, 57.6 us)
Async XLA Ops:
  0.6 109.7 %copy-start = (bf16[512,1024]{1,0:T(8,128)(2,1)S(1)}, bf16[512,1024]{1,0:T(8,128)(2,1)}, u32[]{:S(2)}) copy-start(bf16[512,1024]{1,0:T(8,128)(2,1)} %param.9) | copy-start | bytes 3145732
  1.9 16.9 %collective-permute-start.1 = (bf16[3,32,4096]{2,1,0:T(8,128)(2,1)S(1)}, bf16[3,32,4096]{2,1,0:T(8,128)(2,1)S(1)}, u32[]{:S(2)}, u32[]{:S(2)}) collective-permute-start(bf16[3,32,4096]{2,1,0:T(8,128)(2,1)S(1)} %pad_maximum_fusion.1), channel_id=1, source_target_pairs={{4,0},{8,4},{12,8},{16,12},{20,16},{24,20},{28,24},{32,28},{36,32}... | collective-permute-start | bytes 2359304 | tf_op jit(solution)/shard_map/ppermute | solution.py:21
  9.3 15.4 %collective-permute-start = (bf16[3,32,4096]{2,1,0:T(8,128)(2,1)S(1)}, bf16[3,32,4096]{2,1,0:T(8,128)(2,1)S(1)}, u32[]{:S(2)}, u32[]{:S(2)}) collective-permute-start(bf16[3,32,4096]{2,1,0:T(8,128)(2,1)S(1)} %pad_maximum_fusion.1), channel_id=1, source_target_pairs={{0,4},{4,8},{8,12},{12,16},{16,20},{20,24},{24,28},{28,32},{32,36}... | collective-permute-start | bytes 2359304 | tf_op jit(solution)/shard_map/ppermute | solution.py:20
  30.9 46.3 %all-to-all-start = ((bf16[3,96,4096]{1,0,2:T(4,128)(2,1)}), bf16[3,96,4096]{1,0,2:T(4,128)(2,1)}, u32[]{:S(2)}, u32[]{:S(2)}) async-start(bf16[3,96,4096]{1,0,2:T(4,128)(2,1)} %copy.128), calls=%async_computation | async-start | bytes 8388608 | tf_op jit(solution)/shard_map/all_to_all | solution.py:56
  106.0 36.9 %copy-start.7 = (bf16[48,8,8,128]{3,2,1,0:T(8,128)(2,1)}, bf16[48,8,8,128]{3,2,1,0:T(8,128)(2,1)S(1)}, u32[]{:S(2)}) copy-start(bf16[48,8,8,128]{3,2,1,0:T(8,128)(2,1)S(1)} %copy.171) | copy-start | bytes 2359300
  106.0 35.9 %slice-start.2 = ((s8[6291456]{0:T(1024)(128)(4,1)}), s8[4194304]{0:T(1024)(128)(4,1)S(1)}, s32[]{:S(2)}) async-start(s8[6291456]{0:T(1024)(128)(4,1)} %bitcast.149), calls=%async_computation.3 | async-start | bytes 8388608
  110.4 31.5 %slice-start.3 = ((s8[6291456]{0:T(1024)(128)(4,1)}), s8[2097152]{0:T(1024)(128)(4,1)S(1)}, s32[]{:S(2)}) async-start(s8[6291456]{0:T(1024)(128)(4,1)} %bitcast.149), calls=%async_computation.4 | async-start | bytes 4194304
  116.0 30.9 %collective-permute-start.2 = (f32[8,128]{1,0:T(8,128)S(1)}, f32[8,128]{1,0:T(8,128)S(1)}, u32[]{:S(2)}, u32[]{:S(2)}) collective-permute-start(f32[8,128]{1,0:T(8,128)S(1)} %get-tuple-element.54), channel_id=1, source_target_pairs={{4,0},{8,4},{12,8},{16,12},{20,16},{24,20},{28,24},{32,28},{36,32}... | collective-permute-start | bytes 12296 | tf_op jit(solution)/shard_map/ppermute | solution.py:29
  125.3 23.6 %collective-permute-start.4 = (f32[8,128]{1,0:T(8,128)S(1)}, f32[8,128]{1,0:T(8,128)S(1)}, u32[]{:S(2)}, u32[]{:S(2)}) collective-permute-start(f32[8,128]{1,0:T(8,128)S(1)} %get-tuple-element.55), channel_id=1, source_target_pairs={{0,4},{4,8},{8,12},{12,16},{16,20},{20,24},{24,28},{28,32},{32,36}... | collective-permute-start | bytes 12296 | tf_op jit(solution)/shard_map/ppermute | solution.py:29
  127.2 21.7 %collective-permute-start.3 = (f32[8,128]{1,0:T(8,128)S(1)}, f32[8,128]{1,0:T(8,128)S(1)}, u32[]{:S(2)}, u32[]{:S(2)}) collective-permute-start(f32[8,128]{1,0:T(8,128)S(1)} %get-tuple-element.52), channel_id=1, source_target_pairs={{4,0},{8,4},{12,8},{16,12},{20,16},{24,20},{28,24},{32,28},{36,32}... | collective-permute-start | bytes 12296 | tf_op jit(solution)/shard_map/ppermute | solution.py:29
  132.9 15.9 %collective-permute-start.5 = (f32[8,128]{1,0:T(8,128)S(1)}, f32[8,128]{1,0:T(8,128)S(1)}, u32[]{:S(2)}, u32[]{:S(2)}) collective-permute-start(f32[8,128]{1,0:T(8,128)S(1)} %get-tuple-element.53), channel_id=1, source_target_pairs={{0,4},{4,8},{8,12},{12,16},{16,20},{20,24},{24,28},{28,32},{32,36}... | collective-permute-start | bytes 12296 | tf_op jit(solution)/shard_map/ppermute | solution.py:29
  135.9 48.0 %collective-permute-start.6 = (f32[128,8,128]{0,2,1:T(8,128)}, f32[128,8,128]{0,2,1:T(8,128)}, u32[]{:S(2)}, u32[]{:S(2)}) collective-permute-start(f32[128,8,128]{0,2,1:T(8,128)} %get-tuple-element.43), channel_id=1, source_target_pairs={{4,0},{8,4},{12,8},{16,12},{20,16},{24,20},{28,24},{32,28},{36,32}... | collective-permute-start | bytes 1572872 | tf_op jit(solution)/shard_map/ppermute | solution.py:29
  143.7 31.6 %copy-start.10 = (bf16[384,8,128]{0,2,1:T(8,128)(2,1)S(1)}, bf16[384,8,128]{0,2,1:T(8,128)(2,1)}, u32[]{:S(2)}) copy-start(bf16[384,8,128]{0,2,1:T(8,128)(2,1)} %copy.149) | copy-start | bytes 2359300
  146.9 37.1 %collective-permute-start.7 = (f32[128,8,128]{0,2,1:T(8,128)}, f32[128,8,128]{0,2,1:T(8,128)}, u32[]{:S(2)}, u32[]{:S(2)}) collective-permute-start(f32[128,8,128]{0,2,1:T(8,128)} %get-tuple-element.44), channel_id=1, source_target_pairs={{0,4},{4,8},{8,12},{12,16},{16,20},{20,24},{24,28},{28,32},{32,36}... | collective-permute-start | bytes 1572872 | tf_op jit(solution)/shard_map/ppermute | solution.py:29
  148.9 16.7 %collective-permute-start.11 = (f32[8,128]{1,0:T(8,128)S(1)}, f32[8,128]{1,0:T(8,128)S(1)}, u32[]{:S(2)}, u32[]{:S(2)}) collective-permute-start(f32[8,128]{1,0:T(8,128)S(1)} %get-tuple-element.50), channel_id=1, source_target_pairs={{4,0},{8,4},{12,8},{16,12},{20,16},{24,20},{28,24},{32,28},{36,32}... | collective-permute-start | bytes 12296 | tf_op jit(solution)/shard_map/ppermute | solution.py:21
  154.7 12.9 %collective-permute-start.10 = (f32[8,128]{1,0:T(8,128)S(1)}, f32[8,128]{1,0:T(8,128)S(1)}, u32[]{:S(2)}, u32[]{:S(2)}) collective-permute-start(f32[8,128]{1,0:T(8,128)S(1)} %get-tuple-element.50), channel_id=1, source_target_pairs={{0,4},{4,8},{8,12},{12,16},{16,20},{20,24},{24,28},{28,32},{32,36}... | collective-permute-start | bytes 12296 | tf_op jit(solution)/shard_map/ppermute | solution.py:20
  159.9 33.4 %collective-permute-start.16 = (bf16[128,8,128]{0,2,1:T(8,128)(2,1)}, bf16[128,8,128]{0,2,1:T(8,128)(2,1)}, u32[]{:S(2)}, u32[]{:S(2)}) collective-permute-start(bf16[128,8,128]{0,2,1:T(8,128)(2,1)} %get-tuple-element.45), channel_id=1, source_target_pairs={{4,0},{8,4},{12,8},{16,12},{20,16},{24,20},{28,24},{32,28},{36,32}... | collective-permute-start | bytes 786440 | tf_op jit(solution)/shard_map/ppermute | solution.py:29
  165.6 7.7 %collective-permute-start.8 = (f32[8,128]{1,0:T(8,128)S(1)}, f32[8,128]{1,0:T(8,128)S(1)}, u32[]{:S(2)}, u32[]{:S(2)}) collective-permute-start(f32[8,128]{1,0:T(8,128)S(1)} %get-tuple-element.39), channel_id=1, source_target_pairs={{0,4},{4,8},{8,12},{12,16},{16,20},{20,24},{24,28},{28,32},{32,36}... | collective-permute-start | bytes 12296 | tf_op jit(solution)/shard_map/ppermute | solution.py:20
  167.6 7.7 %collective-permute-start.9 = (f32[8,128]{1,0:T(8,128)S(1)}, f32[8,128]{1,0:T(8,128)S(1)}, u32[]{:S(2)}, u32[]{:S(2)}) collective-permute-start(f32[8,128]{1,0:T(8,128)S(1)} %get-tuple-element.39), channel_id=1, source_target_pairs={{4,0},{8,4},{12,8},{16,12},{20,16},{24,20},{28,24},{32,28},{36,32}... | collective-permute-start | bytes 12296 | tf_op jit(solution)/shard_map/ppermute | solution.py:21
  173.3 19.9 %collective-permute-start.17 = (bf16[128,8,128]{0,2,1:T(8,128)(2,1)}, bf16[128,8,128]{0,2,1:T(8,128)(2,1)}, u32[]{:S(2)}, u32[]{:S(2)}) collective-permute-start(bf16[128,8,128]{0,2,1:T(8,128)(2,1)} %get-tuple-element.46), channel_id=1, source_target_pairs={{0,4},{4,8},{8,12},{12,16},{16,20},{20,24},{24,28},{28,32},{32,36}... | collective-permute-start | bytes 786440 | tf_op jit(solution)/shard_map/ppermute | solution.py:29
  185.6 10.7 %collective-permute-start.13 = (f32[8,128]{1,0:T(8,128)S(1)}, f32[8,128]{1,0:T(8,128)S(1)}, u32[]{:S(2)}, u32[]{:S(2)}) collective-permute-start(f32[8,128]{1,0:T(8,128)S(1)} %bitcast.181), channel_id=1, source_target_pairs={{4,0},{8,4},{12,8},{16,12},{20,16},{24,20},{28,24},{32,28},{36,32}... | collective-permute-start | bytes 12296 | tf_op jit(solution)/shard_map/ppermute | solution.py:21
  191.3 7.0 %collective-permute-start.12 = (f32[8,128]{1,0:T(8,128)S(1)}, f32[8,128]{1,0:T(8,128)S(1)}, u32[]{:S(2)}, u32[]{:S(2)}) collective-permute-start(f32[8,128]{1,0:T(8,128)S(1)} %bitcast.182), channel_id=1, source_target_pairs={{0,4},{4,8},{8,12},{12,16},{16,20},{20,24},{24,28},{28,32},{32,36}... | collective-permute-start | bytes 12296 | tf_op jit(solution)/shard_map/ppermute | solution.py:20
  209.0 7.7 %collective-permute-start.14 = (bf16[128,8,128]{0,2,1:T(8,128)(2,1)S(1)}, bf16[128,8,128]{0,2,1:T(8,128)(2,1)S(1)}, u32[]{:S(2)}, u32[]{:S(2)}) collective-permute-start(bf16[128,8,128]{0,2,1:T(8,128)(2,1)S(1)} %get-tuple-element.47), channel_id=1, source_target_pairs={{4,0},{8,4},{12,8},{16,12},{20,16},{24,20},{28,24},{32,28},{36,32}... | collective-permute-start | bytes 786440 | tf_op jit(solution)/shard_map/ppermute | solution.py:29
  212.7 9.8 %collective-permute-start.15 = (bf16[128,8,128]{0,2,1:T(8,128)(2,1)S(1)}, bf16[128,8,128]{0,2,1:T(8,128)(2,1)S(1)}, u32[]{:S(2)}, u32[]{:S(2)}) collective-permute-start(bf16[128,8,128]{0,2,1:T(8,128)(2,1)S(1)} %get-tuple-element.48), channel_id=1, source_target_pairs={{0,4},{4,8},{8,12},{12,16},{16,20},{20,24},{24,28},{28,32},{32,36}... | collective-permute-start | bytes 786440 | tf_op jit(solution)/shard_map/ppermute | solution.py:29
  (18 other events, 211.7 us)
where the time goes:
time: 226 us; the launch traced here: 224 us
  starting transfers between devices  77.2 us (34%)
  waiting for transfers between devices  59 us (26%)
  matrix products  37.3 us (17%)
  local copies, waits for them, and re-layouts  36.6 us (16%)
  other arithmetic  13 us (6%)
    ppermute x10, starting transfers between devices, from_behind(): return lax.ppermute(block, axis, route)  39.9 us
    all_to_all x1, waiting for transfers between devices, on_device(): lax.all_to_all(window, 'text', split_axis=2, concat_axis=1, tiled=True)  37.6 us
    ppermute x4, starting transfers between devices, extended(): after = lax.ppermute(initial, axis, down)  24.6 us
    unnamed x57, local copies, waits for them, and re-layouts  12.1 us
    dot_general x1, matrix products, on_device(): jnp.einsum('fhd,thd->hft', frame_g, values_win, preferred_element_type=jn...  8.24 us
    ppermute x4, waiting for transfers between devices, extended(): before = lax.ppermute(last, axis, up)  8.03 us
    ppermute x4, starting transfers between devices, extended(): before = lax.ppermute(last, axis, up)  7.68 us
    ppermute x4, waiting for transfers between devices, extended(): after = lax.ppermute(initial, axis, down)  7.57 us
  transfers between devices with their start and end apart: 19, of which 5 were waited for; matrix products, arithmetic and copies ran while one was open for 13% of the time, Pallas kernels for 0%

commit v1 on v0

--- a/solution.py
+++ b/solution.py
@@ -53,7 +53,10 @@
     group_count = lax.axis_size("text")
     rows_sub = stacked.shape[1]
     window = extended(stacked, (("frame", 1),), rows_sub)
-    arrived = lax.all_to_all(window, "text", split_axis=2, concat_axis=1, tiled=True)
+    arrived = jnp.concatenate(
+        lax.all_to_all(jnp.stack(jnp.split(window, lax.axis_size("text"), axis=2)), "text", 0, 0),
+        axis=1,
+    )
     head_width = arrived.shape[2]
     arrived = arrived.reshape(3, group_count, 3, rows_sub, head_width).transpose(0, 2, 1, 3, 4)
     own_rows = group_count * rows_sub

time: 226 us -> 189 us (0.84)
  waiting for transfers between devices: 59 us -> 39.7 us
  local copies, waits for them, and re-layouts: 36.6 us -> 25.7 us
  starting transfers between devices: 77.2 us -> 70.4 us
    all_to_all x1, waiting for transfers between devices: 37.6 us -> 22.1 us  [on_device(): lax.all_to_all(jnp.stack(jnp.split(window, lax.axis_size('text'), axis=2)...]
    ppermute x10, starting transfers between devices: 39.9 us -> 33.7 us  [from_behind(): return lax.ppermute(block, axis, route)]
    ppermute x4, waiting for transfers between devices: 7.57 us -> 1.76 us  [extended(): after = lax.ppermute(initial, axis, down)]
    all_to_all x1, local copies, waits for them, and re-layouts: 5.47 us -> 0.28 us  [on_device(): lax.all_to_all(jnp.stack(jnp.split(window, lax.axis_size('text'), axis=2)...]
    concatenate x1 -> x0, local copies, waits for them, and re-layouts: 4.75 us -> none  [extended(): array = jnp.concatenate([before, array, after], axis=dim)]
    dot_general x1, matrix products: 5.5 us -> 3.04 us  [on_device(): jnp.einsum('fhd,thd->hft', frame_k, keys_win, preferred_element_type=jnp....]
    reduce_sum x1, other arithmetic: 4.32 us -> 2.02 us  [on_device(): col_total = jnp.sum(col_exp, axis=1)]
    ppermute x10, waiting for transfers between devices: 5.85 us -> 8.11 us  [from_behind(): return lax.ppermute(block, axis, route)]
  transfers between devices with their start and end apart: 19 -> 19, of which waited for: 5 -> 5; matrix products, arithmetic and copies ran while one was open for 13% -> 20% of each run, Pallas kernels for 0% -> 0%
where the time goes in v1:
time: 189 us; the launch traced here: 188 us
  starting transfers between devices  70.4 us (37%)
  waiting for transfers between devices  39.7 us (21%)
  matrix products  38.4 us (20%)
  local copies, waits for them, and re-layouts  25.7 us (14%)
  other arithmetic  12.4 us (7%)
    ppermute x10, starting transfers between devices, from_behind(): return lax.ppermute(block, axis, route)  33.7 us
    ppermute x4, starting transfers between devices, extended(): after = lax.ppermute(initial, axis, down)  24.6 us
    all_to_all x1, waiting for transfers between devices, on_device(): lax.all_to_all(jnp.stack(jnp.split(window, lax.axis_size('text'), axis=2)...  22.1 us
    unnamed x47, local copies, waits for them, and re-layouts  13.2 us
    dot_general x1, matrix products, on_device(): jnp.einsum('fhd,thd->hft', frame_g, values_win, preferred_element_type=jn...  8.24 us
    ppermute x10, waiting for transfers between devices, from_behind(): return lax.ppermute(block, axis, route)  8.11 us
    sub x1, matrix products, on_device(): scores - row_max[:, :, None]  7.92 us
    ppermute x4, waiting for transfers between devices, extended(): before = lax.ppermute(last, axis, up)  7.74 us
  transfers between devices with their start and end apart: 19, of which 5 were waited for; matrix products, arithmetic and copies ran while one was open for 20% of the time, Pallas kernels for 0%

profile of v1, /device:TPU:24, one launch (start us, length us, event | category | flops | bytes accessed | tf_op | source)
XLA Modules:
  0.0 187.8 jit_solution(5245905996809524340)
XLA Ops:
  3.9 7.4 %collective-permute-start.1 = (bf16[3,32,4096]{2,1,0:T(8,128)(2,1)S(1)}, bf16[3,32,4096]{2,1,0:T(8,128)(2,1)S(1)}, u32[]{:S(2)}, u32[]{:S(2)}) collective-permute-start(bf16[3,32,4096]{2,1,0:T(8,128)(2,1)S(1)} %pad_maximum_fusion.2), channel_id=1, source_target_pairs={{4,0},{8,4},{12,8},{16,12},{20,16},{24,20},{28,24},{32,28},{36,32}... | collective-permute-start | bytes 2359304 | tf_op jit(solution)/shard_map/ppermute | solution.py:21
  11.3 7.7 %collective-permute-done = bf16[3,32,4096]{2,1,0:T(8,128)(2,1)S(1)} collective-permute-done((bf16[3,32,4096]{2,1,0:T(8,128)(2,1)S(1)}, bf16[3,32,4096]{2,1,0:T(8,128)(2,1)S(1)}, u32[]{:S(2)}, u32[]{:S(2)}) %collective-permute-start) | collective-permute-done | bytes 786464 | tf_op jit(solution)/shard_map/ppermute | solution.py:20
  24.0 4.3 %all-to-all-start = ((bf16[4,3,96,1024]{3,2,1,0:T(8,128)(2,1)}), bf16[4,3,96,1024]{3,2,1,0:T(8,128)(2,1)S(1)}, u32[]{:S(2)}, u32[]{:S(2)}) async-start(bf16[4,3,96,1024]{3,2,1,0:T(8,128)(2,1)} %pad_maximum_fusion.1), calls=%async_computation | async-start | bytes 4718592 | tf_op jit(solution)/shard_map/all_to_all | solution.py:57
  29.4 2.3 %copy.131 = bf16[512,1024]{0,1:T(8,128)(2,1)} copy(bf16[512,1024]{1,0:T(8,128)(2,1)} %param.8) | data formatting | bytes 2097152 | tf_op jit(solution)/shard_map/reshape | solution.py:72
  31.7 2.3 %copy.102 = bf16[512,1024]{0,1:T(8,128)(2,1)} copy(bf16[512,1024]{1,0:T(8,128)(2,1)} %param.10) | data formatting | bytes 2097152 | tf_op args[2]
  34.0 22.1 %all-to-all-done = bf16[4,3,96,1024]{3,2,1,0:T(8,128)(2,1)S(1)} async-done(((bf16[4,3,96,1024]{3,2,1,0:T(8,128)(2,1)}), bf16[4,3,96,1024]{3,2,1,0:T(8,128)(2,1)S(1)}, u32[]{:S(2)}, u32[]{:S(2)}) %all-to-all-start) | async-done | bytes 2359328 | tf_op jit(solution)/shard_map/all_to_all | solution.py:57
  58.9 2.4 %copy.110 = bf16[384,8,128]{0,2,1:T(8,128)(2,1)} copy(bf16[384,8,128]{2,1,0:T(8,128)(2,1)} %bitcast.157) | data formatting | bytes 1572864 | tf_op jit(solution)/shard_map/reshape;squeeze | solution.py:68
  61.3 7.9 %fusion.67 = (f32[8,512]{1,0:T(8,128)S(1)}, f32[8,512,384]{1,2,0:T(8,128)}) fusion(pred[512,384]{0,1:T(8,128)(4,1)} %bitcast.165, bf16[384,8,128]{0,2,1:T(8,128)(2,1)} %copy.110, bf16[512,8,128]{0,2,1:T(8,128)(2,1)} %bitcast.148), kind=kOutput, calls=%fused_computation.97 | convolution fusion | flops 814743936 | bytes 8339456 | tf_op jit(solution)/shard_map/sub | solution.py:83
  69.2 3.0 %fusion.10 = (f32[8,384]{1,0:T(8,128)S(1)}, f32[8,384,512]{2,1,0:T(8,128)S(1)}) fusion(pred[512,384]{0,1:T(8,128)(4,1)} %bitcast.166, bf16[384,8,128]{0,2,1:T(8,128)(2,1)} %copy.110, bf16[512,8,128]{0,2,1:T(8,128)(2,1)} %bitcast.149), kind=kOutput, calls=%fused_computation.16 | convolution fusion | flops 407368704 | bytes 8335360 | tf_op jit(solution)/shard_map/fhd,thd->hft/dot_general | solution.py:79
  74.3 2.2 %fusion.69 = (bf16[384,8,128]{0,2,1:T(8,128)(2,1)S(1)}, f32[384,8,128]{0,2,1:T(8,128)}) fusion(bf16[8,512,384]{1,2,0:T(8,128)(2,1)S(1)} %fusion.26, bf16[512,8,128]{0,2,1:T(8,128)(2,1)S(1)} %bitcast.152), kind=kOutput, calls=%fused_computation.99 | convolution fusion | flops 403046400 | bytes 6553600 | tf_op jit(solution)/shard_map/hft,fhd->thd/dot_general | solution.py:148
  77.5 6.4 %collective-permute-start.16 = (bf16[128,8,128]{0,2,1:T(8,128)(2,1)}, bf16[128,8,128]{0,2,1:T(8,128)(2,1)}, u32[]{:S(2)}, u32[]{:S(2)}) collective-permute-start(bf16[128,8,128]{0,2,1:T(8,128)(2,1)} %get-tuple-element.43), channel_id=1, source_target_pairs={{4,0},{8,4},{12,8},{16,12},{20,16},{24,20},{28,24},{32,28},{36,32}... | collective-permute-start | bytes 786440 | tf_op jit(solution)/shard_map/ppermute | solution.py:29
  87.9 2.4 %collective-permute-start.4 = (f32[8,128]{1,0:T(8,128)S(1)}, f32[8,128]{1,0:T(8,128)S(1)}, u32[]{:S(2)}, u32[]{:S(2)}) collective-permute-start(f32[8,128]{1,0:T(8,128)S(1)} %get-tuple-element.53), channel_id=1, source_target_pairs={{0,4},{4,8},{8,12},{12,16},{16,20},{20,24},{24,28},{28,32},{32,36}... | collective-permute-start | bytes 12296 | tf_op jit(solution)/shard_map/ppermute | solution.py:29
  90.3 5.3 %collective-permute-start.3 = (f32[8,128]{1,0:T(8,128)S(1)}, f32[8,128]{1,0:T(8,128)S(1)}, u32[]{:S(2)}, u32[]{:S(2)}) collective-permute-start(f32[8,128]{1,0:T(8,128)S(1)} %get-tuple-element.50), channel_id=1, source_target_pairs={{4,0},{8,4},{12,8},{16,12},{20,16},{24,20},{28,24},{32,28},{36,32}... | collective-permute-start | bytes 12296 | tf_op jit(solution)/shard_map/ppermute | solution.py:29
  105.7 4.8 %fusion.34 = f32[8,384,512]{2,1,0:T(8,128)} fusion(bf16[384,8,128]{0,2,1:T(8,128)(2,1)} %copy.112, bf16[512,1024]{1,0:T(8,128)(2,1)S(1)} %copy-done), kind=kOutput, calls=%fused_computation.43 | convolution fusion | flops 402653184 | bytes 8126464 | tf_op jit(solution)/shard_map/fhd,thd->hft/dot_general | solution.py:130
  114.9 5.8 %collective-permute-start.6 = (f32[128,8,128]{0,2,1:T(8,128)}, f32[128,8,128]{0,2,1:T(8,128)}, u32[]{:S(2)}, u32[]{:S(2)}) collective-permute-start(f32[128,8,128]{0,2,1:T(8,128)} %get-tuple-element.41), channel_id=1, source_target_pairs={{4,0},{8,4},{12,8},{16,12},{20,16},{24,20},{28,24},{32,28},{36,32}... | collective-permute-start | bytes 1572872 | tf_op jit(solution)/shard_map/ppermute | solution.py:29
  122.7 5.8 %collective-permute-start.9 = (f32[8,128]{1,0:T(8,128)S(1)}, f32[8,128]{1,0:T(8,128)S(1)}, u32[]{:S(2)}, u32[]{:S(2)}) collective-permute-start(f32[8,128]{1,0:T(8,128)S(1)} %get-tuple-element.33), channel_id=1, source_target_pairs={{4,0},{8,4},{12,8},{16,12},{20,16},{24,20},{28,24},{32,28},{36,32}... | collective-permute-start | bytes 12296 | tf_op jit(solution)/shard_map/ppermute | solution.py:21
  130.4 5.8 %collective-permute-start.11 = (f32[8,128]{1,0:T(8,128)S(1)}, f32[8,128]{1,0:T(8,128)S(1)}, u32[]{:S(2)}, u32[]{:S(2)}) collective-permute-start(f32[8,128]{1,0:T(8,128)S(1)} %get-tuple-element.48), channel_id=1, source_target_pairs={{4,0},{8,4},{12,8},{16,12},{20,16},{24,20},{28,24},{32,28},{36,32}... | collective-permute-start | bytes 12296 | tf_op jit(solution)/shard_map/ppermute | solution.py:21
  138.1 6.3 %fusion.27 = bf16[8,128,512]{2,1,0:T(8,128)(2,1)} fusion(bf16[384,8,128]{0,2,1:T(8,128)(2,1)S(1)} %copy-done.12, f32[8,384,512]{2,1,0:T(8,128)} %copy-done.2, f32[8,384]{1,0:T(8,128)S(1)} %compare_select_fusion, f32[8,384]{1,0:T(8,128)S(1)} %pad_maximum_fusion.3, pred[512,384]{0,1:T(8,128)(4,1)} %bitcast.167), kind=kOutput, calls=%fused_computation.38 | convolution fusion | flops 411041792 | bytes 8347648 | tf_op jit(solution)/shard_map/hft,thd->fhd/dot_general | solution.py:139
  144.4 2.4 %copy.120 = bf16[512,1024]{1,0:T(8,128)(2,1)} copy(bf16[512,1024]{0,1:T(8,128)(2,1)} %bitcast.174) | data formatting | bytes 2097152
  146.8 2.3 %collective-permute-done.7 = f32[128,8,128]{0,2,1:T(8,128)} collective-permute-done((f32[128,8,128]{0,2,1:T(8,128)}, f32[128,8,128]{0,2,1:T(8,128)}, u32[]{:S(2)}, u32[]{:S(2)}) %collective-permute-start.7) | collective-permute-done | bytes 524320 | tf_op jit(solution)/shard_map/ppermute | solution.py:29
  152.6 5.8 %collective-permute-start.13 = (f32[8,128]{1,0:T(8,128)S(1)}, f32[8,128]{1,0:T(8,128)S(1)}, u32[]{:S(2)}, u32[]{:S(2)}) collective-permute-start(f32[8,128]{1,0:T(8,128)S(1)} %bitcast.185), channel_id=1, source_target_pairs={{4,0},{8,4},{12,8},{16,12},{20,16},{24,20},{28,24},{32,28},{36,32}... | collective-permute-start | bytes 12296 | tf_op jit(solution)/shard_map/ppermute | solution.py:21
  161.4 8.2 %fusion.2 = bf16[8,512,384]{1,2,0:T(8,128)(2,1)S(1)} fusion(f32[8,384,512]{2,1,0:T(8,128)} %fusion.34, f32[8,384]{1,0:T(8,128)S(1)} %pad_maximum_fusion.4, f32[8,512]{1,0:T(8,128)S(1)} %bitcast.183, bf16[512,8,128]{0,2,1:T(8,128)(2,1)S(1)} %bitcast.153, f32[8,512,384]{1,2,0:T(8,128)} %get-tuple-element.55, f32[8,512]{1,0:T(8,128)S(1)} %get-tuple-element.54, ...), kind=kOutput, calls=%fused_computation.3 | convolution fusion | flops 419954688 | bytes 24121344 | tf_op jit(solution)/shard_map/fhd,thd->hft/dot_general | solution.py:129
  172.0 4.0 %collective-permute-start.14 = (bf16[128,8,128]{0,2,1:T(8,128)(2,1)S(1)}, bf16[128,8,128]{0,2,1:T(8,128)(2,1)S(1)}, u32[]{:S(2)}, u32[]{:S(2)}) collective-permute-start(bf16[128,8,128]{0,2,1:T(8,128)(2,1)S(1)} %get-tuple-element.45), channel_id=1, source_target_pairs={{4,0},{8,4},{12,8},{16,12},{20,16},{24,20},{28,24},{32,28},{36,32}... | collective-permute-start | bytes 786440 | tf_op jit(solution)/shard_map/ppermute | solution.py:29
  180.0 5.8 %collective-permute-done.15 = bf16[128,8,128]{0,2,1:T(8,128)(2,1)S(1)} collective-permute-done((bf16[128,8,128]{0,2,1:T(8,128)(2,1)S(1)}, bf16[128,8,128]{0,2,1:T(8,128)(2,1)S(1)}, u32[]{:S(2)}, u32[]{:S(2)}) %collective-permute-start.15) | collective-permute-done | bytes 262176 | tf_op jit(solution)/shard_map/ppermute | solution.py:29
  (105 shorter events, 53.9 us)
Async XLA Ops:
  0.6 97.2 %copy-start = (bf16[512,1024]{1,0:T(8,128)(2,1)S(1)}, bf16[512,1024]{1,0:T(8,128)(2,1)}, u32[]{:S(2)}) copy-start(bf16[512,1024]{1,0:T(8,128)(2,1)} %param.9) | copy-start | bytes 3145732
  1.9 17.1 %collective-permute-start = (bf16[3,32,4096]{2,1,0:T(8,128)(2,1)S(1)}, bf16[3,32,4096]{2,1,0:T(8,128)(2,1)S(1)}, u32[]{:S(2)}, u32[]{:S(2)}) collective-permute-start(bf16[3,32,4096]{2,1,0:T(8,128)(2,1)S(1)} %pad_maximum_fusion.2), channel_id=1, source_target_pairs={{0,4},{4,8},{8,12},{12,16},{16,20},{20,24},{24,28},{28,32},{32,36}... | collective-permute-start | bytes 2359304 | tf_op jit(solution)/shard_map/ppermute | solution.py:20
  3.9 16.9 %collective-permute-start.1 = (bf16[3,32,4096]{2,1,0:T(8,128)(2,1)S(1)}, bf16[3,32,4096]{2,1,0:T(8,128)(2,1)S(1)}, u32[]{:S(2)}, u32[]{:S(2)}) collective-permute-start(bf16[3,32,4096]{2,1,0:T(8,128)(2,1)S(1)} %pad_maximum_fusion.2), channel_id=1, source_target_pairs={{4,0},{8,4},{12,8},{16,12},{20,16},{24,20},{28,24},{32,28},{36,32}... | collective-permute-start | bytes 2359304 | tf_op jit(solution)/shard_map/ppermute | solution.py:21
  24.0 32.0 %all-to-all-start = ((bf16[4,3,96,1024]{3,2,1,0:T(8,128)(2,1)}), bf16[4,3,96,1024]{3,2,1,0:T(8,128)(2,1)S(1)}, u32[]{:S(2)}, u32[]{:S(2)}) async-start(bf16[4,3,96,1024]{3,2,1,0:T(8,128)(2,1)} %pad_maximum_fusion.1), calls=%async_computation | async-start | bytes 4718592 | tf_op jit(solution)/shard_map/all_to_all | solution.py:57
  72.3 25.6 %copy-start.2 = (f32[8,384,512]{2,1,0:T(8,128)}, f32[8,384,512]{2,1,0:T(8,128)S(1)}, u32[]{:S(2)}) copy-start(f32[8,384,512]{2,1,0:T(8,128)S(1)} %get-tuple-element.57) | copy-start | bytes 18874372
  77.5 80.9 %collective-permute-start.16 = (bf16[128,8,128]{0,2,1:T(8,128)(2,1)}, bf16[128,8,128]{0,2,1:T(8,128)(2,1)}, u32[]{:S(2)}, u32[]{:S(2)}) collective-permute-start(bf16[128,8,128]{0,2,1:T(8,128)(2,1)} %get-tuple-element.43), channel_id=1, source_target_pairs={{4,0},{8,4},{12,8},{16,12},{20,16},{24,20},{28,24},{32,28},{36,32}... | collective-permute-start | bytes 786440 | tf_op jit(solution)/shard_map/ppermute | solution.py:29
  86.0 27.0 %collective-permute-start.2 = (f32[8,128]{1,0:T(8,128)S(1)}, f32[8,128]{1,0:T(8,128)S(1)}, u32[]{:S(2)}, u32[]{:S(2)}) collective-permute-start(f32[8,128]{1,0:T(8,128)S(1)} %get-tuple-element.52), channel_id=1, source_target_pairs={{4,0},{8,4},{12,8},{16,12},{20,16},{24,20},{28,24},{32,28},{36,32}... | collective-permute-start | bytes 12296 | tf_op jit(solution)/shard_map/ppermute | solution.py:29
  87.9 27.0 %collective-permute-start.4 = (f32[8,128]{1,0:T(8,128)S(1)}, f32[8,128]{1,0:T(8,128)S(1)}, u32[]{:S(2)}, u32[]{:S(2)}) collective-permute-start(f32[8,128]{1,0:T(8,128)S(1)} %get-tuple-element.53), channel_id=1, source_target_pairs={{0,4},{4,8},{8,12},{12,16},{16,20},{20,24},{24,28},{28,32},{32,36}... | collective-permute-start | bytes 12296 | tf_op jit(solution)/shard_map/ppermute | solution.py:29
  90.3 30.4 %collective-permute-start.3 = (f32[8,128]{1,0:T(8,128)S(1)}, f32[8,128]{1,0:T(8,128)S(1)}, u32[]{:S(2)}, u32[]{:S(2)}) collective-permute-start(f32[8,128]{1,0:T(8,128)S(1)} %get-tuple-element.50), channel_id=1, source_target_pairs={{4,0},{8,4},{12,8},{16,12},{20,16},{24,20},{28,24},{32,28},{36,32}... | collective-permute-start | bytes 12296 | tf_op jit(solution)/shard_map/ppermute | solution.py:29
  95.6 25.1 %collective-permute-start.5 = (f32[8,128]{1,0:T(8,128)S(1)}, f32[8,128]{1,0:T(8,128)S(1)}, u32[]{:S(2)}, u32[]{:S(2)}) collective-permute-start(f32[8,128]{1,0:T(8,128)S(1)} %get-tuple-element.51), channel_id=1, source_target_pairs={{0,4},{4,8},{8,12},{12,16},{16,20},{20,24},{24,28},{28,32},{32,36}... | collective-permute-start | bytes 12296 | tf_op jit(solution)/shard_map/ppermute | solution.py:29
  105.6 32.5 %copy-start.12 = (bf16[384,8,128]{0,2,1:T(8,128)(2,1)S(1)}, bf16[384,8,128]{0,2,1:T(8,128)(2,1)}, u32[]{:S(2)}) copy-start(bf16[384,8,128]{0,2,1:T(8,128)(2,1)} %copy.112) | copy-start | bytes 2359300
  113.0 45.4 %collective-permute-start.17 = (bf16[128,8,128]{0,2,1:T(8,128)(2,1)}, bf16[128,8,128]{0,2,1:T(8,128)(2,1)}, u32[]{:S(2)}, u32[]{:S(2)}) collective-permute-start(bf16[128,8,128]{0,2,1:T(8,128)(2,1)} %get-tuple-element.44), channel_id=1, source_target_pairs={{0,4},{4,8},{8,12},{12,16},{16,20},{20,24},{24,28},{28,32},{32,36}... | collective-permute-start | bytes 786440 | tf_op jit(solution)/shard_map/ppermute | solution.py:29
  114.9 31.9 %collective-permute-start.6 = (f32[128,8,128]{0,2,1:T(8,128)}, f32[128,8,128]{0,2,1:T(8,128)}, u32[]{:S(2)}, u32[]{:S(2)}) collective-permute-start(f32[128,8,128]{0,2,1:T(8,128)} %get-tuple-element.41), channel_id=1, source_target_pairs={{4,0},{8,4},{12,8},{16,12},{20,16},{24,20},{28,24},{32,28},{36,32}... | collective-permute-start | bytes 1572872 | tf_op jit(solution)/shard_map/ppermute | solution.py:29
  120.7 7.7 %collective-permute-start.8 = (f32[8,128]{1,0:T(8,128)S(1)}, f32[8,128]{1,0:T(8,128)S(1)}, u32[]{:S(2)}, u32[]{:S(2)}) collective-permute-start(f32[8,128]{1,0:T(8,128)S(1)} %get-tuple-element.33), channel_id=1, source_target_pairs={{0,4},{4,8},{8,12},{12,16},{16,20},{20,24},{24,28},{28,32},{32,36}... | collective-permute-start | bytes 12296 | tf_op jit(solution)/shard_map/ppermute | solution.py:20
  122.7 7.7 %collective-permute-start.9 = (f32[8,128]{1,0:T(8,128)S(1)}, f32[8,128]{1,0:T(8,128)S(1)}, u32[]{:S(2)}, u32[]{:S(2)}) collective-permute-start(f32[8,128]{1,0:T(8,128)S(1)} %get-tuple-element.33), channel_id=1, source_target_pairs={{4,0},{8,4},{12,8},{16,12},{20,16},{24,20},{28,24},{32,28},{36,32}... | collective-permute-start | bytes 12296 | tf_op jit(solution)/shard_map/ppermute | solution.py:21
  128.4 7.7 %collective-permute-start.10 = (f32[8,128]{1,0:T(8,128)S(1)}, f32[8,128]{1,0:T(8,128)S(1)}, u32[]{:S(2)}, u32[]{:S(2)}) collective-permute-start(f32[8,128]{1,0:T(8,128)S(1)} %get-tuple-element.48), channel_id=1, source_target_pairs={{0,4},{4,8},{8,12},{12,16},{16,20},{20,24},{24,28},{28,32},{32,36}... | collective-permute-start | bytes 12296 | tf_op jit(solution)/shard_map/ppermute | solution.py:20
  130.4 7.7 %collective-permute-start.11 = (f32[8,128]{1,0:T(8,128)S(1)}, f32[8,128]{1,0:T(8,128)S(1)}, u32[]{:S(2)}, u32[]{:S(2)}) collective-permute-start(f32[8,128]{1,0:T(8,128)S(1)} %get-tuple-element.48), channel_id=1, source_target_pairs={{4,0},{8,4},{12,8},{16,12},{20,16},{24,20},{28,24},{32,28},{36,32}... | collective-permute-start | bytes 12296 | tf_op jit(solution)/shard_map/ppermute | solution.py:21
  136.2 12.9 %collective-permute-start.7 = (f32[128,8,128]{0,2,1:T(8,128)}, f32[128,8,128]{0,2,1:T(8,128)}, u32[]{:S(2)}, u32[]{:S(2)}) collective-permute-start(f32[128,8,128]{0,2,1:T(8,128)} %get-tuple-element.42), channel_id=1, source_target_pairs={{0,4},{4,8},{8,12},{12,16},{16,20},{20,24},{24,28},{28,32},{32,36}... | collective-permute-start | bytes 1572872 | tf_op jit(solution)/shard_map/ppermute | solution.py:29
  144.4 17.0 %copy-start.14 = (pred[48,8,4,128]{3,1,2,0:T(8,128)(4,1)S(1)}, pred[48,8,4,128]{3,1,2,0:T(8,128)(4,1)}, u32[]{:S(2)}) copy-start(pred[48,8,4,128]{3,1,2,0:T(8,128)(4,1)} %copy.152) | copy-start | bytes 589828
  150.7 10.7 %collective-permute-start.12 = (f32[8,128]{1,0:T(8,128)S(1)}, f32[8,128]{1,0:T(8,128)S(1)}, u32[]{:S(2)}, u32[]{:S(2)}) collective-permute-start(f32[8,128]{1,0:T(8,128)S(1)} %bitcast.184), channel_id=1, source_target_pairs={{0,4},{4,8},{8,12},{12,16},{16,20},{20,24},{24,28},{28,32},{32,36}... | collective-permute-start | bytes 12296 | tf_op jit(solution)/shard_map/ppermute | solution.py:20
  152.6 8.8 %collective-permute-start.13 = (f32[8,128]{1,0:T(8,128)S(1)}, f32[8,128]{1,0:T(8,128)S(1)}, u32[]{:S(2)}, u32[]{:S(2)}) collective-permute-start(f32[8,128]{1,0:T(8,128)S(1)} %bitcast.185), channel_id=1, source_target_pairs={{4,0},{8,4},{12,8},{16,12},{20,16},{24,20},{28,24},{32,28},{36,32}... | collective-permute-start | bytes 12296 | tf_op jit(solution)/shard_map/ppermute | solution.py:21
  169.7 18.2 %copy-start.1 = (bf16[512,1024]{1,0:T(8,128)(2,1)S(1)}, bf16[512,1024]{1,0:T(8,128)(2,1)}, u32[]{:S(2)}) copy-start(bf16[512,1024]{1,0:T(8,128)(2,1)} %param.9) | copy-start | bytes 3145732
  172.0 8.0 %collective-permute-start.14 = (bf16[128,8,128]{0,2,1:T(8,128)(2,1)S(1)}, bf16[128,8,128]{0,2,1:T(8,128)(2,1)S(1)}, u32[]{:S(2)}, u32[]{:S(2)}) collective-permute-start(bf16[128,8,128]{0,2,1:T(8,128)(2,1)S(1)} %get-tuple-element.45), channel_id=1, source_target_pairs={{4,0},{8,4},{12,8},{16,12},{20,16},{24,20},{28,24},{32,28},{36,32}... | collective-permute-start | bytes 786440 | tf_op jit(solution)/shard_map/ppermute | solution.py:29
  176.0 9.8 %collective-permute-start.15 = (bf16[128,8,128]{0,2,1:T(8,128)(2,1)S(1)}, bf16[128,8,128]{0,2,1:T(8,128)(2,1)S(1)}, u32[]{:S(2)}, u32[]{:S(2)}) collective-permute-start(bf16[128,8,128]{0,2,1:T(8,128)(2,1)S(1)} %get-tuple-element.46), channel_id=1, source_target_pairs={{0,4},{4,8},{8,12},{12,16},{16,20},{20,24},{24,28},{28,32},{32,36}... | collective-permute-start | bytes 786440 | tf_op jit(solution)/shard_map/ppermute | solution.py:29
  (13 other events, 95.0 us)
